TPU v7x, 32 devices: a whole 2x2x4 slice. The times are simulated.
32 devices in a mesh: grp: 2 (over y), seq: 4 (over z), head: 4 (over x, core).
Axes of the slice: x: 2, y: 2, z: 4, core: 2. Of those that a mesh axis runs over, the one named last changes fastest.
Arguments:
- queries: bfloat16 [5120, 8192], P(('grp', 'seq'), 'head'), parts along dimension 0, may hold values from -30 to 30, as said below
- keys: bfloat16 [5120, 8192], P(('grp', 'seq'), 'head'), parts along dimension 0, may hold values from -6 to 6
- values: bfloat16 [5120, 8192], P(('grp', 'seq'), 'head'), parts along dimension 0, may hold values from -24 to 24, as said below
- gain: bfloat16 [8192], P('head'), may hold values from 0.25 to 1.75
Outputs:
- output: bfloat16 [5120, 8192], P(('grp', 'seq'), 'head'), parts along dimension 0
There are 2 independent parts, one for each index of `grp`. A program takes and returns all parts, laid end to end along the dimension named above; an argument that names none is the same for every part. Nothing has to cross between parts.
Inputs may be any that keep to these rules, and one draw needn't show every extreme that they name: `queries`: query rows of various sizes. `values`: value features and rows of various sizes.
All inputs are finite; a program needn't handle non-finite values.
Results may differ from a plain program's by a relative error of at most 0.0051.
Values sent between devices are 32-bit elements; how exact they have to be, the bound alone decides.
No kernel may reach another device: no remote copies, remote signals or barrier semaphores. Data moves between devices by JAX's collectives and lax.ppermute only.
A program may use at most 64 MiB of HBM per device.

v0:
```python
import jax
import jax.numpy as jnp
from jax import lax
from jax.sharding import PartitionSpec as P

HEADS = 64
HEAD_DIM = 128


def body(queries, keys, values, gain):
    tokens_here = queries.shape[0]
    heads_here = queries.shape[1] // HEAD_DIM
    queries_split = queries.reshape(tokens_here, heads_here, HEAD_DIM)
    keys_split = keys.reshape(tokens_here, heads_here, HEAD_DIM)
    values_split = values.reshape(tokens_here, heads_here, HEAD_DIM)
    local_state = jnp.einsum(
        "thd,the->hde", keys_split, values_split, preferred_element_type=jnp.float32
    )
    my_index = lax.axis_index("seq")
    piece = lax.all_gather(local_state[None], "seq", axis=0, tiled=True)
    owners = jnp.arange(piece.shape[0], dtype=jnp.int32)
    weights = (owners < my_index).astype(jnp.float32)
    prefix = jnp.sum(piece * weights[:, None, None, None], axis=0)
    positions = jnp.arange(tokens_here)
    causal = positions[:, None] >= positions[None, :]
    scores = jnp.einsum(
        "thd,shd->hts", queries_split, keys_split, preferred_element_type=jnp.float32
    )
    scores = jnp.where(causal[None], scores, jnp.float32(0.0)).astype(jnp.bfloat16)
    intra_term = jnp.einsum(
        "hts,she->the", scores, values_split, preferred_element_type=jnp.float32
    )
    prefix_low = prefix.astype(jnp.bfloat16)
    inter_term = jnp.einsum(
        "thd,hde->the", queries_split, prefix_low, preferred_element_type=jnp.float32
    )
    mixed = (intra_term + inter_term).reshape(tokens_here, heads_here * HEAD_DIM)
    partial_squares = jnp.sum(mixed * mixed, axis=1)
    total_squares = lax.psum(partial_squares, "head")
    factor = lax.rsqrt(total_squares / (HEADS * HEAD_DIM) + 1e-06)
    return (mixed * factor[:, None] * gain.astype(jnp.float32)[None, :]).astype(jnp.bfloat16)


def solution(mesh):
    placed = (
        P(("grp", "seq"), "head"),
        P(("grp", "seq"), "head"),
        P(("grp", "seq"), "head"),
        P("head"),
    )
    return jax.shard_map(
        body, mesh=mesh, in_specs=placed, out_specs=P(("grp", "seq"), "head"), check_vma=False
    )
```

profile of v0, /device:TPU:0, one launch (start us, length us, event | category | flops | bytes accessed | tf_op | source)
XLA Modules:
  0.0 132.1 jit_solution(14653907628350191327)
XLA Ops:
  6.5 0.0 copy-start
  6.5 0.0 all-gather.3.cloned.1.call-start
  6.5 4.5 %copy.17 = bf16[640,2048]{0,1:T(8,128)(2,1)} copy(bf16[640,2048]{1,0:T(8,128)(2,1)} %param.5) | data formatting | bytes 5242880 | tf_op jit(solution)/shard_map/reshape | solution.py:14
  11.1 0.0 copy-start.1
  11.1 4.4 %fusion.2 = f32[16,128,128]{2,1,0:T(8,128)} fusion(bf16[640,16,128]{0,2,1:T(8,128)(2,1)} %bitcast.43, bf16[640,2048]{1,0:T(8,128)(2,1)} %param.6), kind=kOutput, calls=%fused_computation.7 | convolution fusion | flops 335544320 | bytes 6291456 | tf_op jit(solution)/shard_map/thd,the->hde/dot_general | solution.py:16
  15.4 0.0 all-gather.3.cloned.1.call-update
  15.5 0.0 copy-done.1
  15.5 0.1 iota_compare_fusion
  15.6 0.0 copy-done
  15.6 10.9 %fusion = f32[16,640,128]{1,2,0:T(8,128)} fusion(bf16[640,16,128]{0,2,1:T(8,128)(2,1)} %bitcast.44, pred[640,640]{1,0:T(8,128)(4,1)S(1)} %iota_compare_fusion, bf16[640,2048]{1,0:T(8,128)(2,1)} %param.6, bf16[640,2048]{1,0:T(8,128)(2,1)S(1)} %copy-done), kind=kOutput, calls=%fused_computation.5 | convolution fusion | flops 3368550400 | bytes 13516800 | tf_op jit(solution)/shard_map/hts,she->the/dot_general | solution.py:30
  26.5 72.6 %all-gather.3.cloned.1.call-done = f32[64,128,128]{2,1,0:T(8,128)} async-done(((f32[16,128,128]{2,1,0:T(8,128)}), f32[64,128,128]{2,1,0:T(8,128)}) %all-gather.3.cloned.1.call-update) | async-done | bytes 4194320 | tf_op jit(solution)/shard_map/all_gather | solution.py:20
  99.1 2.7 %multiply_reduce_fusion.1 = bf16[16,128,128]{2,1,0:T(8,128)(2,1)S(1)} fusion(f32[4,16,128,128]{3,2,1,0:T(8,128)} %bitcast.42, f32[4]{0:T(128)S(1)} %compare_convert_fusion), kind=kLoop, calls=%fused_computation.4 | loop fusion | flops 1835008 | bytes 4718608 | tf_op jit(solution)/shard_map/reduce_sum | solution.py:23
  101.8 6.0 %multiply_reduce_fusion = (f32[640]{0:T(1024)S(1)}, f32[640,16,128]{0,2,1:T(8,128)}) fusion(bf16[16,128,128]{2,1,0:T(8,128)(2,1)S(1)} %multiply_reduce_fusion.1, f32[16,640,128]{1,2,0:T(8,128)} %fusion, bf16[640,2048]{1,0:T(8,128)(2,1)S(1)} %copy-done), kind=kOutput, calls=%fused_computation.3 | convolution fusion | flops 339475840 | bytes 13634048 | tf_op jit(solution)/shard_map/thd,hde->the/dot_general | solution.py:34
  107.8 6.0 %copy.15 = f32[640,2048]{1,0:T(8,128)} copy(f32[640,2048]{0,1:T(8,128)} %bitcast.41) | data formatting | bytes 10485760 | tf_op jit(solution)/shard_map/reshape | solution.py:37
  113.9 6.9 %psum.7 = f32[640]{0:T(1024)S(1)} all-reduce(f32[640]{0:T(1024)S(1)} %get-tuple-element.5), channel_id=1, replica_groups=mesh['grp'=2,'seq'=4,'head'=4] {'head'}, use_global_device_ids=true, to_apply=%region_2.3 | all-reduce | flops 640 | bytes 5120 | tf_op jit(solution)/shard_map/psum | solution.py:39
  120.7 4.5 %multiply_convert_fusion = bf16[640,2048]{1,0:T(8,128)(2,1)} fusion(f32[640,2048]{1,0:T(8,128)} %copy.15, f32[2048]{0:T(1024)S(1)} %convert_element_type.22, f32[640]{0:T(1024)S(1)} %add_rsqrt_fusion), kind=kLoop, calls=%fused_computation.2 | loop fusion | flops 3932160 | bytes 7875072 | tf_op jit(solution)/shard_map/convert_element_type | solution.py:41
  (3 shorter events, 0.0 us)
Async XLA Ops:
  6.5 9.1 %copy-start = (bf16[640,2048]{1,0:T(8,128)(2,1)S(1)}, bf16[640,2048]{1,0:T(8,128)(2,1)}, u32[]{:S(2)}) copy-start(bf16[640,2048]{1,0:T(8,128)(2,1)} %param.4) | copy-start | bytes 7864324
  6.5 92.5 %all-gather.3.cloned.1.call-start = ((), (), s32[]{:S(2)}) async-start(), calls=%async_computation | async-start | bytes 5242880 | tf_op jit(solution)/shard_map/all_gather | solution.py:20
  11.1 4.4 %copy-start.1 = (bf16[2048]{0:T(1024)(128)(2,1)S(1)}, bf16[2048]{0:T(1024)(128)(2,1)}, u32[]{:S(2)}) copy-start(bf16[2048]{0:T(1024)(128)(2,1)} %param.7) | copy-start | bytes 12292
Sparse Core Ops, SparseCore 0:
  15.6 83.4 all-gather.2
where the time goes:
time: 132 us
  waiting for transfers between devices  72.6 us (55%)
  matrix products  21.3 us (16%)
  between operations  13.4 us (10%)
  local copies, waits for them, and re-layouts  10.6 us (8%)
  other arithmetic  7.33 us (6%)
  blocking collectives  6.86 us (5%)
    all_gather x1, waiting for transfers between devices, body(): piece = lax.all_gather(local_state[None], 'seq', axis=0, tiled=True)  72.6 us
    dot_general x1, matrix products, body(): jnp.einsum('hts,she->the', scores, values_split, preferred_element_type=j...  10.9 us
    psum x1, blocking collectives, body(): total_squares = lax.psum(partial_squares, 'head')  6.86 us
    reshape x1, local copies, waits for them, and re-layouts, body(): (intra_term + inter_term).reshape(tokens_here, heads_here * HEAD_DIM)  6.05 us
    dot_general x1, matrix products, body(): jnp.einsum('thd,hde->the', queries_split, prefix_low, preferred_element_t...  6.03 us
    reshape x1, local copies, waits for them, and re-layouts, body(): keys_split = keys.reshape(tokens_here, heads_here, HEAD_DIM)  4.52 us
    convert_element_type x1, other arithmetic, body(): (mixed * factor[:, None] * gain.astype(jnp.float32)[None, :]).astype(jnp....  4.47 us
    dot_general x1, matrix products, body(): jnp.einsum('thd,the->hde', keys_split, values_split, preferred_element_ty...  4.37 us
  transfers between devices with their start and end apart: 1, of which 1 were waited for; matrix products, arithmetic and copies ran while one was open for 8% of the time, Pallas kernels for 0%

commit v1 on v0

--- a/solution.py
+++ b/solution.py
@@ -5,6 +5,12 @@
 
 HEADS = 64
 HEAD_DIM = 128
+
+
+def in_order(blocks, dim):
+    dims = list(blocks.shape[1:])
+    dims[dim] *= blocks.shape[0]
+    return jnp.moveaxis(blocks, 0, dim).reshape(dims)
 
 
 def body(queries, keys, values, gain):
@@ -17,7 +23,14 @@
         "thd,the->hde", keys_split, values_split, preferred_element_type=jnp.float32
     )
     my_index = lax.axis_index("seq")
-    piece = lax.all_gather(local_state[None], "seq", axis=0, tiled=True)
+    devices = lax.axis_size("seq")
+    right = [(i, (i + 1) % devices) for i in range(devices)]
+    blocks = [local_state[None]]
+    while len(blocks) < devices:
+        blocks.append(lax.ppermute(blocks[-1], "seq", right))
+    index = lax.axis_index("seq")
+    blocks = jnp.stack(blocks)[(index - jnp.arange(devices)) % devices]
+    piece = in_order(blocks, 0)
     owners = jnp.arange(piece.shape[0], dtype=jnp.int32)
     weights = (owners < my_index).astype(jnp.float32)
     prefix = jnp.sum(piece * weights[:, None, None, None], axis=0)

time: 132 us -> 124 us (0.939)
  between operations: 13.4 us -> 0.06 us
  waiting for transfers between devices: 72.6 us -> 66.2 us
  local copies, waits for them, and re-layouts: 10.6 us -> 16.7 us
  other arithmetic: 7.33 us -> 12 us
  starting transfers between devices: 0.01 us -> 3.03 us
    all_gather x1 -> x0, waiting for transfers between devices: 72.6 us -> none  [body(): piece = lax.all_gather(local_state[None], 'seq', axis=0, tiled=True)]
    ppermute x0 -> x3, waiting for transfers between devices: none -> 66.2 us  [body(): blocks.append(lax.ppermute(blocks[-1], 'seq', right))]
    gather x0 -> x1, local copies, waits for them, and re-layouts: none -> 5.07 us  [body(): blocks = jnp.stack(blocks)[(index - jnp.arange(devices)) % devices]]
    another operation x0 -> x1, other arithmetic: none -> 4.68 us  [body(): blocks = jnp.stack(blocks)[(index - jnp.arange(devices)) % devices]]
    ppermute x0 -> x3, starting transfers between devices: none -> 3.03 us  [body(): blocks.append(lax.ppermute(blocks[-1], 'seq', right))]
  transfers between devices with their start and end apart: 1 -> 3, of which waited for: 1 -> 3; matrix products, arithmetic and copies ran while one was open for 8% -> 9% of each run, Pallas kernels for 0% -> 0%
where the time goes in v1:
time: 124 us
  waiting for transfers between devices  66.2 us (53%)
  matrix products  20.3 us (16%)
  local copies, waits for them, and re-layouts  16.7 us (13%)
  other arithmetic  12 us (10%)
  blocking collectives  5.63 us (5%)
  starting transfers between devices  3.03 us (2%)
    ppermute x3, waiting for transfers between devices, body(): blocks.append(lax.ppermute(blocks[-1], 'seq', right))  66.2 us
    dot_general x1, matrix products, body(): jnp.einsum('hts,she->the', scores, values_split, preferred_element_type=j...  10.9 us
    reshape x1, local copies, waits for them, and re-layouts, body(): (intra_term + inter_term).reshape(tokens_here, heads_here * HEAD_DIM)  6.05 us
    dot_general x1, matrix products, body(): jnp.einsum('thd,hde->the', queries_split, prefix_low, preferred_element_t...  6.03 us
    psum x1, blocking collectives, body(): total_squares = lax.psum(partial_squares, 'head')  5.63 us
    gather x1, local copies, waits for them, and re-layouts, body(): blocks = jnp.stack(blocks)[(index - jnp.arange(devices)) % devices]  5.07 us
    another operation x1, other arithmetic, body(): blocks = jnp.stack(blocks)[(index - jnp.arange(devices)) % devices]  4.68 us
    reshape x1, local copies, waits for them, and re-layouts, body(): keys_split = keys.reshape(tokens_here, heads_here, HEAD_DIM)  4.52 us
  transfers between devices with their start and end apart: 3, of which 3 were waited for; matrix products, arithmetic and copies ran while one was open for 9% of the time, Pallas kernels for 0%

profile of v1, /device:TPU:0, one launch (start us, length us, event | category | flops | bytes accessed | tf_op | source)
XLA Modules:
  0.0 123.9 jit_solution(13571764012517201591)
XLA Ops:
  0.0 0.0 copy-start
  0.0 4.5 %copy.17 = bf16[640,2048]{0,1:T(8,128)(2,1)} copy(bf16[640,2048]{1,0:T(8,128)(2,1)} %param.5) | data formatting | bytes 5242880 | tf_op jit(solution)/shard_map/reshape | solution.py:20
  4.5 0.0 copy-start.2
  4.5 3.4 %fusion.2 = f32[16,128,128]{2,1,0:T(8,128)S(1)} fusion(bf16[640,16,128]{0,2,1:T(8,128)(2,1)} %bitcast.50, bf16[640,2048]{1,0:T(8,128)(2,1)} %param.6), kind=kOutput, calls=%fused_computation.9 | convolution fusion | flops 335544320 | bytes 6291456 | tf_op jit(solution)/shard_map/thd,the->hde/dot_general | solution.py:22
  7.9 0.0 copy-start.1
  7.9 1.0 copy-done.1
  9.0 3.0 %collective-permute-start = (f32[1,16,128,128]{3,2,1,0:T(8,128)S(1)}, f32[1,16,128,128]{3,2,1,0:T(8,128)}, u32[]{:S(2)}, u32[]{:S(2)}) collective-permute-start(f32[1,16,128,128]{3,2,1,0:T(8,128)S(1)} %bitcast.52), channel_id=1, source_target_pairs={{0,4},{4,8},{8,12},{12,0},{1,5},{5,9},{9,13},{13,1},{2,6},{6,10},{... | collective-permute-start | bytes 3145736 | tf_op jit(solution)/shard_map/ppermute | solution.py:30
  12.0 25.3 %collective-permute-done = f32[1,16,128,128]{3,2,1,0:T(8,128)} collective-permute-done((f32[1,16,128,128]{3,2,1,0:T(8,128)S(1)}, f32[1,16,128,128]{3,2,1,0:T(8,128)}, u32[]{:S(2)}, u32[]{:S(2)}) %collective-permute-start) | collective-permute-done | bytes 1048608 | tf_op jit(solution)/shard_map/ppermute | solution.py:30
  37.3 0.0 collective-permute-start.1
  37.3 0.0 copy-done.2
  37.4 0.1 iota_compare_fusion
  37.5 26.3 %collective-permute-done.1 = f32[1,16,128,128]{3,2,1,0:T(8,128)} collective-permute-done((f32[1,16,128,128]{3,2,1,0:T(8,128)}, f32[1,16,128,128]{3,2,1,0:T(8,128)}, u32[]{:S(2)}, u32[]{:S(2)}) %collective-permute-start.1) | collective-permute-done | bytes 1048608 | tf_op jit(solution)/shard_map/ppermute | solution.py:30
  63.8 0.0 collective-permute-start.2
  63.8 0.0 copy-done
  63.8 10.9 %fusion = f32[16,640,128]{1,2,0:T(8,128)} fusion(bf16[640,16,128]{0,2,1:T(8,128)(2,1)} %bitcast.51, pred[640,640]{1,0:T(8,128)(4,1)S(1)} %iota_compare_fusion, bf16[640,2048]{1,0:T(8,128)(2,1)} %param.6, bf16[640,2048]{1,0:T(8,128)(2,1)S(1)} %copy-done), kind=kOutput, calls=%fused_computation.7 | convolution fusion | flops 3368550400 | bytes 13516800 | tf_op jit(solution)/shard_map/hts,she->the/dot_general | solution.py:43
  74.6 14.7 %collective-permute-done.2 = f32[1,16,128,128]{3,2,1,0:T(8,128)} collective-permute-done((f32[1,16,128,128]{3,2,1,0:T(8,128)}, f32[1,16,128,128]{3,2,1,0:T(8,128)}, u32[]{:S(2)}, u32[]{:S(2)}) %collective-permute-start.2) | collective-permute-done | bytes 1048608 | tf_op jit(solution)/shard_map/ppermute | solution.py:30
  89.3 4.7 %maximum_bitcast_fusion = f32[4,16,128,128]{3,2,1,0:T(8,128)} fusion(f32[1,1,16,128,128]{4,3,2,1,0:T(8,128)} %bitcast.6, f32[1,1,16,128,128]{4,3,2,1,0:T(8,128)} %bitcast.5, f32[1,1,16,128,128]{4,3,2,1,0:T(8,128)} %bitcast.4, f32[1,1,16,128,128]{4,3,2,1,0:T(8,128)} %bitcast.53), kind=kLoop, calls=%fused_computation.5 | loop fusion | flops 3145728 | bytes 8388608 | tf_op jit(solution)/shard_map/stack | solution.py:32
  94.0 5.1 %gather_fusion = f32[4,16,128,128]{3,2,1,0:T(8,128)} fusion(f32[4,16,128,128]{3,2,1,0:T(8,128)} %maximum_bitcast_fusion, s32[1024]{0:T(1024)S(1)} %pad_clamp_fusion), kind=kCustom, calls=%fused_computation | custom fusion | bytes 8388624 | tf_op jit(solution)/shard_map/gather | solution.py:32
  99.0 2.7 %multiply_reduce_fusion.1 = bf16[16,128,128]{2,1,0:T(8,128)(2,1)S(1)} fusion(f32[4,16,128,128]{3,2,1,0:T(8,128)} %gather_fusion, f32[4]{0:T(128)S(1)} %compare_convert_fusion), kind=kLoop, calls=%fused_computation.6 | loop fusion | flops 1835008 | bytes 4718608 | tf_op jit(solution)/shard_map/reduce_sum | solution.py:36
  101.8 6.0 %multiply_reduce_fusion = (f32[640]{0:T(1024)S(1)}, f32[640,16,128]{0,2,1:T(8,128)}) fusion(bf16[16,128,128]{2,1,0:T(8,128)(2,1)S(1)} %multiply_reduce_fusion.1, f32[16,640,128]{1,2,0:T(8,128)} %fusion, bf16[640,2048]{1,0:T(8,128)(2,1)S(1)} %copy-done), kind=kOutput, calls=%fused_computation.4 | convolution fusion | flops 339475840 | bytes 13634048 | tf_op jit(solution)/shard_map/thd,hde->the/dot_general | solution.py:47
  107.8 6.0 %copy.15 = f32[640,2048]{1,0:T(8,128)} copy(f32[640,2048]{0,1:T(8,128)} %bitcast.49) | data formatting | bytes 10485760 | tf_op jit(solution)/shard_map/reshape | solution.py:50
  113.8 5.6 %psum.7 = f32[640]{0:T(1024)S(1)} all-reduce(f32[640]{0:T(1024)S(1)} %get-tuple-element.5), channel_id=1, replica_groups=mesh['grp'=2,'seq'=4,'head'=4] {'head'}, use_global_device_ids=true, to_apply=%region_2.3 | all-reduce | flops 640 | bytes 5120 | tf_op jit(solution)/shard_map/psum | solution.py:52
  119.5 4.5 %multiply_convert_fusion = bf16[640,2048]{1,0:T(8,128)(2,1)} fusion(f32[640,2048]{1,0:T(8,128)} %copy.15, f32[2048]{0:T(1024)S(1)} %convert_element_type.22, f32[640]{0:T(1024)S(1)} %add_rsqrt_fusion), kind=kLoop, calls=%fused_computation.3 | loop fusion | flops 3932160 | bytes 7875072 | tf_op jit(solution)/shard_map/convert_element_type | solution.py:54
  (5 shorter events, 0.0 us)
Async XLA Ops:
  0.0 63.8 %copy-start = (bf16[640,2048]{1,0:T(8,128)(2,1)S(1)}, bf16[640,2048]{1,0:T(8,128)(2,1)}, u32[]{:S(2)}) copy-start(bf16[640,2048]{1,0:T(8,128)(2,1)} %param.4) | copy-start | bytes 7864324
  4.5 32.8 %copy-start.2 = (bf16[2048]{0:T(1024)(128)(2,1)S(1)}, bf16[2048]{0:T(1024)(128)(2,1)}, u32[]{:S(2)}) copy-start(bf16[2048]{0:T(1024)(128)(2,1)} %param.7) | copy-start | bytes 12292
  7.9 1.1 copy-start.1
  9.0 28.3 %collective-permute-start = (f32[1,16,128,128]{3,2,1,0:T(8,128)S(1)}, f32[1,16,128,128]{3,2,1,0:T(8,128)}, u32[]{:S(2)}, u32[]{:S(2)}) collective-permute-start(f32[1,16,128,128]{3,2,1,0:T(8,128)S(1)} %bitcast.52), channel_id=1, source_target_pairs={{0,4},{4,8},{8,12},{12,0},{1,5},{5,9},{9,13},{13,1},{2,6},{6,10},{... | collective-permute-start | bytes 3145736 | tf_op jit(solution)/shard_map/ppermute | solution.py:30
  37.3 26.5 %collective-permute-start.1 = (f32[1,16,128,128]{3,2,1,0:T(8,128)}, f32[1,16,128,128]{3,2,1,0:T(8,128)}, u32[]{:S(2)}, u32[]{:S(2)}) collective-permute-start(f32[1,16,128,128]{3,2,1,0:T(8,128)} %collective-permute-done), channel_id=1, source_target_pairs={{0,4},{4,8},{8,12},{12,0},{1,5},{5,9},{9,13},{13,1},{2,6},{6,10},{... | collective-permute-start | bytes 3145736 | tf_op jit(solution)/shard_map/ppermute | solution.py:30
  63.8 25.5 %collective-permute-start.2 = (f32[1,16,128,128]{3,2,1,0:T(8,128)}, f32[1,16,128,128]{3,2,1,0:T(8,128)}, u32[]{:S(2)}, u32[]{:S(2)}) collective-permute-start(f32[1,16,128,128]{3,2,1,0:T(8,128)} %collective-permute-done.1), channel_id=1, source_target_pairs={{0,4},{4,8},{8,12},{12,0},{1,5},{5,9},{9,13},{13,1},{2,6},{6,10},{... | collective-permute-start | bytes 3145736 | tf_op jit(solution)/shard_map/ppermute | solution.py:30
